TPU v7x, 128 devices: a whole 4x4x4 slice. The times are simulated.
128 devices in a mesh: ctx: 16 (over y_lo, x, core), exp: 8 (over y_hi, z).
Axes of the slice: x: 4, y: 4 (y_hi: 2, y_lo: 2; y = y_hi * 2 + y_lo), z: 4, core: 2. Of those that a mesh axis runs over, the one named last changes fastest.
Arguments:
- queries: bfloat16 [2048, 3072], P('ctx', 'exp'), may hold values from -8 to 8
- keys: bfloat16 [2048, 1024], P('ctx', 'exp'), may hold values from -8 to 8
- values: bfloat16 [2048, 1024], P('ctx', 'exp'), may hold values from -6 to 6
- norm_gain: float32 [3072], replicated, may hold values from 0.1 to 1.9
- routes: int32 [2048, 2], P(('ctx', 'exp')), may hold values from 0 to 7, all different within a row; in each aligned block of 16 rows (0 to 15, 16 to 31, ...) at most 6 rows name the same one
- route_scores: float32 [2048, 2], P(('ctx', 'exp')), may hold values from -8 to 8
- cotangent: bfloat16 [2048, 3072], P(('ctx', 'exp')), may hold values from -6 to 6
- w_gate: bfloat16 [8, 3072, 8192], P('exp', None, 'ctx'), may hold values from -0.109375 to 0.109375
- w_up: bfloat16 [8, 3072, 8192], P('exp', None, 'ctx'), may hold values from -0.109375 to 0.109375
- w_down: bfloat16 [8, 8192, 3072], P('exp', 'ctx'), may hold values from -0.0625 to 0.0625
Outputs:
- mixed: bfloat16 [2048, 3072], P(('ctx', 'exp'))
- grad_input: bfloat16 [2048, 3072], P(('ctx', 'exp'))
- grad_gate: bfloat16 [8, 3072, 8192], P('exp', None, 'ctx')
- grad_up: bfloat16 [8, 3072, 8192], P('exp', None, 'ctx')
- grad_down: bfloat16 [8, 8192, 3072], P('exp', 'ctx')
Inputs may be any that keep to these rules, and one draw needn't show every extreme that they name: `routes`: each row names two different experts. Within each aligned block of 16 rows (the rows of one device) no expert is named by more than 6 rows, a bound that some block reaches.
All inputs are finite; a program needn't handle non-finite values.
Results may differ from a plain program's by a relative error of at most 0.018.
Values may be sent and summed in bfloat16 or wider, within the bound.
A program may use at most 128 MiB of HBM per device.

v0:
```python
import jax
import jax.numpy as jnp
from jax import lax
from jax.sharding import PartitionSpec as P

norm_eps = 1e-05
masked_value = -1e30


def shifted(block, axis, distance):
    devices = range(lax.axis_size(axis))
    route = [(i - distance, i) for i in devices if i - distance in devices]
    return lax.ppermute(block, axis, route)


def heads_first(query_local, group, head):
    count = query_local.shape[0]
    return query_local.reshape(count, group, head).transpose(1, 0, 2).reshape(group * count, head)


def attend_piece(state, query_flat, query_pos, piece, start, head):
    running_max, running_sum, accum = state
    key_part = piece[:, :head]
    value_part = piece[:, head:].astype(jnp.float32)
    scores = lax.dot_general(
        query_flat, key_part, (((1,), (1,)), ((), ())), preferred_element_type=jnp.float32
    ) * head ** (-0.5)
    key_pos = start + jnp.arange(piece.shape[0], dtype=jnp.int32)
    allowed = key_pos[None, :] <= query_pos[:, None]
    scores = jnp.where(allowed, scores, masked_value)
    new_max = jnp.maximum(running_max, jnp.max(scores, axis=1))
    weights = jnp.where(allowed, jnp.exp(scores - new_max[:, None]), 0.0)
    factor = jnp.exp(running_max - new_max)
    new_sum = running_sum * factor + jnp.sum(weights, axis=1)
    product = jnp.dot(
        weights, value_part, precision=lax.Precision.HIGHEST, preferred_element_type=jnp.float32
    )
    new_accum = accum * factor[:, None] + product
    return (new_max, new_sum, new_accum)


def local(queries, keys, values, norm_gain, routes, route_scores, cotangent, w_gate, w_up, w_down):
    n_ctx = lax.axis_size("ctx")
    n_exp = lax.axis_size("exp")
    head = keys.shape[1]
    group = queries.shape[1] // head
    tok_ctx = queries.shape[0]
    ctx_index = lax.axis_index("ctx")
    query_flat = heads_first(queries, group, head)
    query_pos = ctx_index * tok_ctx + jnp.tile(jnp.arange(tok_ctx, dtype=jnp.int32), group)
    key_values = jnp.concatenate([keys, values], axis=1)
    query_rows = query_flat.shape[0]
    initial = (
        jnp.full((query_rows,), masked_value, jnp.float32),
        jnp.zeros((query_rows,), jnp.float32),
        jnp.zeros((query_rows, head), jnp.float32),
    )
    first = attend_piece(initial, query_flat, query_pos, key_values, ctx_index * tok_ctx, head)

    def cycle_step(step, carry):
        state, current = carry
        current = shifted(current, "ctx", 1)
        source = (ctx_index - step) % n_ctx
        state = attend_piece(state, query_flat, query_pos, current, source * tok_ctx, head)
        return (state, current)

    state, _ = lax.fori_loop(1, n_ctx, cycle_step, (first, key_values))
    running_max, running_sum, accum = state
    attended = accum / running_sum[:, None]
    attended = (
        attended.reshape(group, tok_ctx, head)
        .transpose(1, 0, 2)
        .reshape(tok_ctx, group * head)
        .astype(jnp.bfloat16)
    )
    features = lax.all_to_all(attended, "exp", split_axis=0, concat_axis=1, tiled=True)
    feats = features.astype(jnp.float32)
    inv_rms = lax.rsqrt(jnp.mean(feats * feats, axis=1) + norm_eps)
    normed = (feats * inv_rms[:, None] * norm_gain[None, :]).astype(jnp.bfloat16)
    tok_dev = normed.shape[0]
    width = normed.shape[1]
    capacity = 3 * tok_dev // n_exp
    slots = n_exp * capacity
    flat_routes = routes.reshape(-1)
    onehot = (flat_routes[:, None] == jnp.arange(n_exp, dtype=jnp.int32)[None, :]).astype(jnp.int32)
    ranks = jnp.sum((jnp.cumsum(onehot, axis=0) - onehot) * onehot, axis=1)
    target = flat_routes * capacity + ranks
    placed = (jnp.arange(slots, dtype=jnp.int32)[:, None] == target[None, :]).astype(jnp.float32)
    place_tokens = placed.reshape(slots, tok_dev, 2).sum(axis=2)
    probs = jax.nn.softmax(route_scores, axis=1)
    mixing = (placed * probs.reshape(-1)[None, :]).reshape(slots, tok_dev, 2).sum(axis=2)
    send = jnp.dot(
        place_tokens.astype(jnp.bfloat16), normed, preferred_element_type=jnp.float32
    ).astype(jnp.bfloat16)
    arrived = lax.all_to_all(
        send.reshape(n_exp, capacity, width), "exp", split_axis=0, concat_axis=0, tiled=True
    ).reshape(slots, width)
    expert_in = lax.all_gather(arrived, "ctx", axis=0, tiled=True)
    gate_w = w_gate[0]
    up_w = w_up[0]
    down_w = w_down[0]
    gate_pre = jnp.dot(expert_in, gate_w, preferred_element_type=jnp.float32)
    up_pre = jnp.dot(expert_in, up_w, preferred_element_type=jnp.float32)
    hidden = (jax.nn.silu(gate_pre) * up_pre).astype(jnp.bfloat16)
    expert_out = lax.psum_scatter(
        jnp.dot(hidden, down_w, preferred_element_type=jnp.float32).astype(jnp.bfloat16),
        "ctx",
        scatter_dimension=0,
        tiled=True,
    )
    returned = lax.all_to_all(
        expert_out.reshape(n_exp, capacity, width), "exp", split_axis=0, concat_axis=0, tiled=True
    ).reshape(slots, width)
    mixed = lax.dot_general(
        mixing,
        returned.astype(jnp.float32),
        (((0,), (0,)), ((), ())),
        precision=lax.Precision.HIGHEST,
    ).astype(jnp.bfloat16)
    grad_slots = jnp.dot(
        mixing, cotangent.astype(jnp.float32), precision=lax.Precision.HIGHEST
    ).astype(jnp.bfloat16)
    grad_arrived = lax.all_to_all(
        grad_slots.reshape(n_exp, capacity, width), "exp", split_axis=0, concat_axis=0, tiled=True
    ).reshape(slots, width)
    grad_out, rows_in = (
        lax.all_gather(grad_arrived, "ctx", axis=0, tiled=True),
        lax.all_gather(arrived, "ctx", axis=0, tiled=True),
    )
    grad_hidden = lax.dot_general(
        grad_out, down_w, (((1,), (1,)), ((), ())), preferred_element_type=jnp.float32
    )
    grad_down = lax.dot_general(
        hidden, grad_out, (((0,), (0,)), ((), ())), preferred_element_type=jnp.float32
    ).astype(jnp.bfloat16)
    sig = jax.nn.sigmoid(gate_pre)
    grad_up_pre = (grad_hidden * (gate_pre * sig)).astype(jnp.bfloat16)
    grad_gate_pre = (grad_hidden * up_pre * sig * (1.0 + gate_pre * (1.0 - sig))).astype(
        jnp.bfloat16
    )
    grad_gate = lax.dot_general(
        rows_in, grad_gate_pre, (((0,), (0,)), ((), ())), preferred_element_type=jnp.float32
    ).astype(jnp.bfloat16)
    grad_upw = lax.dot_general(
        rows_in, grad_up_pre, (((0,), (0,)), ((), ())), preferred_element_type=jnp.float32
    ).astype(jnp.bfloat16)
    term = lax.dot_general(
        grad_gate_pre, gate_w, (((1,), (1,)), ((), ())), preferred_element_type=jnp.float32
    )
    grad_summed = lax.psum_scatter(
        (
            term
            + lax.dot_general(
                grad_up_pre, up_w, (((1,), (1,)), ((), ())), preferred_element_type=jnp.float32
            )
        ).astype(jnp.bfloat16),
        "ctx",
        scatter_dimension=0,
        tiled=True,
    )
    grad_back = lax.all_to_all(
        grad_summed.reshape(n_exp, capacity, width), "exp", split_axis=0, concat_axis=0, tiled=True
    ).reshape(slots, width)
    grad_normed = lax.dot_general(
        place_tokens,
        grad_back.astype(jnp.float32),
        (((0,), (0,)), ((), ())),
        precision=lax.Precision.HIGHEST,
    )
    weighted = grad_normed * norm_gain[None, :]
    inner = jnp.mean(weighted * feats, axis=1)
    grad_input = (inv_rms[:, None] * weighted - feats * (inv_rms**3 * inner)[:, None]).astype(
        jnp.bfloat16
    )
    return (mixed, grad_input, grad_gate[None], grad_upw[None], grad_down[None])


def solution(mesh):
    placed = (
        P("ctx", "exp"),
        P("ctx", "exp"),
        P("ctx", "exp"),
        P(),
        P(("ctx", "exp"), None),
        P(("ctx", "exp"), None),
        P(("ctx", "exp"), None),
        P("exp", None, "ctx"),
        P("exp", None, "ctx"),
        P("exp", "ctx", None),
    )
    return jax.shard_map(
        local,
        mesh=mesh,
        in_specs=placed,
        out_specs=(
            P(("ctx", "exp"), None),
            P(("ctx", "exp"), None),
            P("exp", None, "ctx"),
            P("exp", None, "ctx"),
            P("exp", "ctx", None),
        ),
        check_vma=False,
    )
```

profile of v0, /device:TPU:16, one launch (start us, length us, event | category | flops | bytes accessed | tf_op | source)
XLA Modules:
  0.0 441.2 jit_solution(11982174086630426389)
XLA Ops:
  7.2 1.2 copy.45
  8.5 1.4 pad_maximum_fusion
  11.0 1.2 convolution_add_fusion.1
  12.2 109.1 %while.22 = (s32[]{:T(128)}, f32[384]{0:T(512)S(1)}, f32[384]{0:T(512)S(1)}, f32[384,128]{1,0:T(8,128)S(1)}, bf16[128,256]{1,0:T(8,128)(2,1)}, /*index=5*/s32[]{...) while((s32[]{:T(128)}, f32[384]{0:T(512)S(1)}, ...), condition=%wide.region_11.12_spmd.clone, body=%wide.region_8.11_spmd.clone.sunk | while | flops 88720656 | bytes 1575218 | solution.py:67
  12.2 1.7 collective-permute-start
  16.5 4.2 collective-permute-start
  23.3 4.7 %collective-permute-start = (bf16[128,256]{1,0:T(8,128)(2,1)}, bf16[128,256]{1,0:T(8,128)(2,1)S(1)}, u32[]{:S(2)}, u32[]{:S(2)}) collective-permute-start(bf16[128,256]{1,0:T(8,128)(2,1)} %get-tuple-element.331), channel_id=1, source_target_pairs={{0,8},{8,16},{16,24},{24,32},{32,40},{40,48},{48,56},{56,64},{64,7... | collective-permute-start | bytes 196616 | tf_op jit(solution)/shard_map/while/body/eval_jaxpr/ppermute | solution.py:13
  30.5 4.7 %collective-permute-start = (bf16[128,256]{1,0:T(8,128)(2,1)}, bf16[128,256]{1,0:T(8,128)(2,1)S(1)}, u32[]{:S(2)}, u32[]{:S(2)}) collective-permute-start(bf16[128,256]{1,0:T(8,128)(2,1)} %get-tuple-element.331), channel_id=1, source_target_pairs={{0,8},{8,16},{16,24},{24,32},{32,40},{40,48},{48,56},{56,64},{64,7... | collective-permute-start | bytes 196616 | tf_op jit(solution)/shard_map/while/body/eval_jaxpr/ppermute | solution.py:13
  37.8 4.7 %collective-permute-start = (bf16[128,256]{1,0:T(8,128)(2,1)}, bf16[128,256]{1,0:T(8,128)(2,1)S(1)}, u32[]{:S(2)}, u32[]{:S(2)}) collective-permute-start(bf16[128,256]{1,0:T(8,128)(2,1)} %get-tuple-element.331), channel_id=1, source_target_pairs={{0,8},{8,16},{16,24},{24,32},{32,40},{40,48},{48,56},{56,64},{64,7... | collective-permute-start | bytes 196616 | tf_op jit(solution)/shard_map/while/body/eval_jaxpr/ppermute | solution.py:13
  45.0 4.7 %collective-permute-start = (bf16[128,256]{1,0:T(8,128)(2,1)}, bf16[128,256]{1,0:T(8,128)(2,1)S(1)}, u32[]{:S(2)}, u32[]{:S(2)}) collective-permute-start(bf16[128,256]{1,0:T(8,128)(2,1)} %get-tuple-element.331), channel_id=1, source_target_pairs={{0,8},{8,16},{16,24},{24,32},{32,40},{40,48},{48,56},{56,64},{64,7... | collective-permute-start | bytes 196616 | tf_op jit(solution)/shard_map/while/body/eval_jaxpr/ppermute | solution.py:13
  52.3 4.7 %collective-permute-start = (bf16[128,256]{1,0:T(8,128)(2,1)}, bf16[128,256]{1,0:T(8,128)(2,1)S(1)}, u32[]{:S(2)}, u32[]{:S(2)}) collective-permute-start(bf16[128,256]{1,0:T(8,128)(2,1)} %get-tuple-element.331), channel_id=1, source_target_pairs={{0,8},{8,16},{16,24},{24,32},{32,40},{40,48},{48,56},{56,64},{64,7... | collective-permute-start | bytes 196616 | tf_op jit(solution)/shard_map/while/body/eval_jaxpr/ppermute | solution.py:13
  59.5 4.7 %collective-permute-start = (bf16[128,256]{1,0:T(8,128)(2,1)}, bf16[128,256]{1,0:T(8,128)(2,1)S(1)}, u32[]{:S(2)}, u32[]{:S(2)}) collective-permute-start(bf16[128,256]{1,0:T(8,128)(2,1)} %get-tuple-element.331), channel_id=1, source_target_pairs={{0,8},{8,16},{16,24},{24,32},{32,40},{40,48},{48,56},{56,64},{64,7... | collective-permute-start | bytes 196616 | tf_op jit(solution)/shard_map/while/body/eval_jaxpr/ppermute | solution.py:13
  66.7 4.7 %collective-permute-start = (bf16[128,256]{1,0:T(8,128)(2,1)}, bf16[128,256]{1,0:T(8,128)(2,1)S(1)}, u32[]{:S(2)}, u32[]{:S(2)}) collective-permute-start(bf16[128,256]{1,0:T(8,128)(2,1)} %get-tuple-element.331), channel_id=1, source_target_pairs={{0,8},{8,16},{16,24},{24,32},{32,40},{40,48},{48,56},{56,64},{64,7... | collective-permute-start | bytes 196616 | tf_op jit(solution)/shard_map/while/body/eval_jaxpr/ppermute | solution.py:13
  74.0 4.7 %collective-permute-start = (bf16[128,256]{1,0:T(8,128)(2,1)}, bf16[128,256]{1,0:T(8,128)(2,1)S(1)}, u32[]{:S(2)}, u32[]{:S(2)}) collective-permute-start(bf16[128,256]{1,0:T(8,128)(2,1)} %get-tuple-element.331), channel_id=1, source_target_pairs={{0,8},{8,16},{16,24},{24,32},{32,40},{40,48},{48,56},{56,64},{64,7... | collective-permute-start | bytes 196616 | tf_op jit(solution)/shard_map/while/body/eval_jaxpr/ppermute | solution.py:13
  81.2 4.7 %collective-permute-start = (bf16[128,256]{1,0:T(8,128)(2,1)}, bf16[128,256]{1,0:T(8,128)(2,1)S(1)}, u32[]{:S(2)}, u32[]{:S(2)}) collective-permute-start(bf16[128,256]{1,0:T(8,128)(2,1)} %get-tuple-element.331), channel_id=1, source_target_pairs={{0,8},{8,16},{16,24},{24,32},{32,40},{40,48},{48,56},{56,64},{64,7... | collective-permute-start | bytes 196616 | tf_op jit(solution)/shard_map/while/body/eval_jaxpr/ppermute | solution.py:13
  88.5 4.7 %collective-permute-start = (bf16[128,256]{1,0:T(8,128)(2,1)}, bf16[128,256]{1,0:T(8,128)(2,1)S(1)}, u32[]{:S(2)}, u32[]{:S(2)}) collective-permute-start(bf16[128,256]{1,0:T(8,128)(2,1)} %get-tuple-element.331), channel_id=1, source_target_pairs={{0,8},{8,16},{16,24},{24,32},{32,40},{40,48},{48,56},{56,64},{64,7... | collective-permute-start | bytes 196616 | tf_op jit(solution)/shard_map/while/body/eval_jaxpr/ppermute | solution.py:13
  95.7 4.7 %collective-permute-start = (bf16[128,256]{1,0:T(8,128)(2,1)}, bf16[128,256]{1,0:T(8,128)(2,1)S(1)}, u32[]{:S(2)}, u32[]{:S(2)}) collective-permute-start(bf16[128,256]{1,0:T(8,128)(2,1)} %get-tuple-element.331), channel_id=1, source_target_pairs={{0,8},{8,16},{16,24},{24,32},{32,40},{40,48},{48,56},{56,64},{64,7... | collective-permute-start | bytes 196616 | tf_op jit(solution)/shard_map/while/body/eval_jaxpr/ppermute | solution.py:13
  103.0 6.5 %collective-permute-start = (bf16[128,256]{1,0:T(8,128)(2,1)}, bf16[128,256]{1,0:T(8,128)(2,1)S(1)}, u32[]{:S(2)}, u32[]{:S(2)}) collective-permute-start(bf16[128,256]{1,0:T(8,128)(2,1)} %get-tuple-element.331), channel_id=1, source_target_pairs={{0,8},{8,16},{16,24},{24,32},{32,40},{40,48},{48,56},{56,64},{64,7... | collective-permute-start | bytes 196616 | tf_op jit(solution)/shard_map/while/body/eval_jaxpr/ppermute | solution.py:13
  112.0 6.8 %collective-permute-start = (bf16[128,256]{1,0:T(8,128)(2,1)}, bf16[128,256]{1,0:T(8,128)(2,1)S(1)}, u32[]{:S(2)}, u32[]{:S(2)}) collective-permute-start(bf16[128,256]{1,0:T(8,128)(2,1)} %get-tuple-element.331), channel_id=1, source_target_pairs={{0,8},{8,16},{16,24},{24,32},{32,40},{40,48},{48,56},{56,64},{64,7... | collective-permute-start | bytes 196616 | tf_op jit(solution)/shard_map/while/body/eval_jaxpr/ppermute | solution.py:13
  122.3 8.3 %all-to-all-start = ((bf16[8,16,384]{2,1,0:T(8,128)(2,1)}), bf16[8,16,384]{2,1,0:T(8,128)(2,1)S(1)}, u32[]{:S(2)}, u32[]{:S(2)}) async-start(bf16[8,16,384]{2,1,0:T(8,128)(2,1)} %convert_element_type.88), calls=%async_computation | async-start | bytes 196608 | tf_op jit(solution)/shard_map/all_to_all | solution.py:76
  131.4 4.7 %all-to-all-done = bf16[8,16,384]{2,1,0:T(8,128)(2,1)S(1)} async-done(((bf16[8,16,384]{2,1,0:T(8,128)(2,1)}), bf16[8,16,384]{2,1,0:T(8,128)(2,1)S(1)}, u32[]{:S(2)}, u32[]{:S(2)}) %all-to-all-start) | async-done | bytes 98336 | tf_op jit(solution)/shard_map/all_to_all | solution.py:76
  137.3 1.8 reshape.128
  139.1 13.7 %all_to_all.30 = bf16[8,6,3072]{2,1,0:T(8,128)(2,1)} all-to-all(bf16[8,6,3072]{2,1,0:T(8,128)(2,1)} %reshape.128), channel_id=1, replica_groups=mesh['ctx'=16,'exp'=8] {'exp'}, dimensions={0} | all-to-all | bytes 589824 | tf_op jit(solution)/shard_map/all_to_all | solution.py:95
  152.8 1.8 reshape.129
  155.8 1.8 reshape.132
  157.6 13.6 %all_to_all.31 = bf16[8,6,3072]{2,1,0:T(8,128)(2,1)} all-to-all(bf16[8,6,3072]{2,1,0:T(8,128)(2,1)} %reshape.132), channel_id=1, replica_groups=mesh['ctx'=16,'exp'=8] {'exp'}, dimensions={0} | all-to-all | bytes 589824 | tf_op jit(solution)/shard_map/all_to_all | solution.py:123
  171.2 1.8 reshape.133
  173.1 48.4 %all-gather.3.cloned.1.call-done = bf16[768,3072]{1,0:T(8,128)(2,1)} async-done(((bf16[48,3072]{1,0:T(8,128)(2,1)}), bf16[768,3072]{1,0:T(8,128)(2,1)}) %all-gather.3.cloned.1.call-update) | async-done | bytes 4718608 | tf_op jit(solution)/shard_map/all_gather | solution.py:98
  221.5 7.2 %fusion.18 = f32[768,512]{1,0:T(8,128)} fusion(bf16[768,3072]{1,0:T(8,128)(2,1)} %all-gather.3.cloned.1.call-done, bf16[1,3072,512]{2,1,0:T(8,128)(2,1)} %param.20), kind=kOutput, calls=%fused_computation.33 | convolution fusion | flops 2415919104 | bytes 9437184 | tf_op jit(solution)/shard_map/dot_general | solution.py:103
  228.7 3.7 fusion.22
  232.4 29.6 %all-gather.5.cloned.1.call-done = bf16[768,3072]{1,0:T(8,128)(2,1)} async-done(((bf16[48,3072]{1,0:T(8,128)(2,1)}), bf16[768,3072]{1,0:T(8,128)(2,1)}) %all-gather.5.cloned.1.call-update) | async-done | bytes 4718608 | tf_op jit(solution)/shard_map/all_gather | solution.py:127
  262.0 7.0 %multiply_convert_fusion = (bf16[768,512]{1,0:T(8,128)(2,1)}, bf16[768,512]{1,0:T(8,128)(2,1)}, bf16[768,512]{1,0:T(8,128)(2,1)S(1)}) fusion(f32[768,512]{1,0:T(8,128)} %fusion.22, f32[768,512]{1,0:T(8,128)} %fusion.18, bf16[768,3072]{1,0:T(8,128)(2,1)} %all-gather.5.cloned.1.call-done, bf16[1,512,3072]{2,1,0:T(8,128)(2,1)S(1)} %copy-done), kind=kOutput, calls=%fused_computation.39 | convolution fusion | flops 2421817344 | bytes 13369344 | tf_op jit(solution)/shard_map/dot_general | solution.py:130
  269.9 4.2 convolution_convert_fusion
  274.4 4.9 %fusion.20 = f32[768,3072]{1,0:T(8,128)S(1)} fusion(bf16[768,512]{1,0:T(8,128)(2,1)} %get-tuple-element.249, bf16[1,3072,512]{2,1,0:T(8,128)(2,1)} %param.19), kind=kOutput, calls=%fused_computation.35 | convolution fusion | flops 2415919104 | bytes 13369344 | tf_op jit(solution)/shard_map/dot_general | solution.py:147
  279.4 4.4 %add_convert_fusion = bf16[768,3072]{1,0:T(8,128)(2,1)} fusion(f32[768,3072]{1,0:T(8,128)S(1)} %fusion.20, bf16[768,512]{1,0:T(8,128)(2,1)S(1)} %copy-done.2, bf16[1,3072,512]{2,1,0:T(8,128)(2,1)S(1)} %copy-done.1), kind=kOutput, calls=%fused_computation.17 | convolution fusion | flops 2420637696 | bytes 18087936 | tf_op jit(solution)/shard_map/dot_general | solution.py:153
  283.8 6.9 %fusion.13 = bf16[1,512,3072]{2,1,0:T(8,128)(2,1)} fusion(bf16[768,512]{1,0:T(8,128)(2,1)} %copy-done.9, bf16[768,3072]{1,0:T(8,128)(2,1)} %all-gather.5.cloned.1.call-done), kind=kOutput, calls=%fused_computation.24 | convolution fusion | flops 2417491968 | bytes 8650752 | tf_op jit(solution)/shard_map/dot_general | solution.py:133
  290.7 51.4 %reduce-scatter.3.cloned.1.call-done = bf16[48,3072]{1,0:T(8,128)(2,1)} async-done(((bf16[768,3072]{1,0:T(8,128)(2,1)}), bf16[48,3072]{1,0:T(8,128)(2,1)}) %reduce-scatter.3.cloned.1.call-update) | async-done | bytes 294928 | tf_op jit(solution)/shard_map/reduce_scatter | solution.py:105
  342.1 1.8 reshape.130
  343.9 7.5 %all-to-all-start.2 = ((bf16[8,6,3072]{2,1,0:T(8,128)(2,1)}), bf16[8,6,3072]{2,1,0:T(8,128)(2,1)}, u32[]{:S(2)}, u32[]{:S(2)}) async-start(bf16[8,6,3072]{2,1,0:T(8,128)(2,1)} %reshape.130), calls=%async_computation.3 | async-start | bytes 786432 | tf_op jit(solution)/shard_map/all_to_all | solution.py:111
  351.5 7.0 %fusion.12 = bf16[1,3072,512]{2,1,0:T(8,128)(2,1)} fusion(bf16[768,3072]{1,0:T(8,128)(2,1)} %all-gather.3.cloned.1.call-done, bf16[768,512]{1,0:T(8,128)(2,1)} %get-tuple-element.248), kind=kOutput, calls=%fused_computation.23 | convolution fusion | flops 2417491968 | bytes 8650752 | tf_op jit(solution)/shard_map/dot_general | solution.py:144
  358.5 52.4 %reduce-scatter.5.cloned.1.call-done = bf16[48,3072]{1,0:T(8,128)(2,1)} async-done(((bf16[768,3072]{1,0:T(8,128)(2,1)}), bf16[48,3072]{1,0:T(8,128)(2,1)}) %reduce-scatter.5.cloned.1.call-update) | async-done | bytes 294928 | tf_op jit(solution)/shard_map/reduce_scatter | solution.py:150
  410.9 1.8 reshape.134
  412.7 7.5 %all-to-all-start.4 = ((bf16[8,6,3072]{2,1,0:T(8,128)(2,1)}), bf16[8,6,3072]{2,1,0:T(8,128)(2,1)}, u32[]{:S(2)}, u32[]{:S(2)}) async-start(bf16[8,6,3072]{2,1,0:T(8,128)(2,1)} %reshape.134), calls=%async_computation.6 | async-start | bytes 786432 | tf_op jit(solution)/shard_map/all_to_all | solution.py:161
  420.2 6.9 %fusion.11 = bf16[1,3072,512]{2,1,0:T(8,128)(2,1)} fusion(bf16[768,3072]{1,0:T(8,128)(2,1)} %all-gather.3.cloned.1.call-done, bf16[768,512]{1,0:T(8,128)(2,1)} %get-tuple-element.249), kind=kOutput, calls=%fused_computation.22 | convolution fusion | flops 2417491968 | bytes 8650752 | tf_op jit(solution)/shard_map/dot_general | solution.py:141
  427.1 1.8 reshape.131
  428.9 1.9 convolution_convert_fusion.6
  430.8 1.8 reshape.135
  432.6 1.3 multiply_reduce_fusion
  (210 shorter events, 44.2 us)
Async XLA Ops:
  7.2 254.9 %copy-start = (bf16[1,512,3072]{2,1,0:T(8,128)(2,1)S(1)}, bf16[1,512,3072]{2,1,0:T(8,128)(2,1)}, u32[]{:S(2)}) copy-start(bf16[1,512,3072]{2,1,0:T(8,128)(2,1)} %param.21) | copy-start | bytes 9437188
  12.2 118.4 %copy-start.5 = (f32[16,2]{0,1:T(2,128)S(1)}, f32[16,2]{0,1:T(2,128)}, u32[]{:S(2)}) copy-start(f32[16,2]{0,1:T(2,128)} %param.17) | copy-start | bytes 388
  12.2 118.4 %copy-start.6 = (s32[16,2]{0,1:T(2,128)S(1)}, s32[16,2]{0,1:T(2,128)}, u32[]{:S(2)}) copy-start(s32[16,2]{0,1:T(2,128)} %param.16) | copy-start | bytes 388
  12.2 124.0 %copy-start.4 = (f32[3072]{0:T(1024)S(1)}, f32[3072]{0:T(1024)}, u32[]{:S(2)}) copy-start(f32[3072]{0:T(1024)} %param.15) | copy-start | bytes 36868
  12.2 2.8 collective-permute-start
  16.5 5.3 %collective-permute-start = (bf16[128,256]{1,0:T(8,128)(2,1)}, bf16[128,256]{1,0:T(8,128)(2,1)S(1)}, u32[]{:S(2)}, u32[]{:S(2)}) collective-permute-start(bf16[128,256]{1,0:T(8,128)(2,1)} %get-tuple-element.331), channel_id=1, source_target_pairs={{0,8},{8,16},{16,24},{24,32},{32,40},{40,48},{48,56},{56,64},{64,7... | collective-permute-start | bytes 196616 | tf_op jit(solution)/shard_map/while/body/eval_jaxpr/ppermute | solution.py:13
  23.3 5.8 %collective-permute-start = (bf16[128,256]{1,0:T(8,128)(2,1)}, bf16[128,256]{1,0:T(8,128)(2,1)S(1)}, u32[]{:S(2)}, u32[]{:S(2)}) collective-permute-start(bf16[128,256]{1,0:T(8,128)(2,1)} %get-tuple-element.331), channel_id=1, source_target_pairs={{0,8},{8,16},{16,24},{24,32},{32,40},{40,48},{48,56},{56,64},{64,7... | collective-permute-start | bytes 196616 | tf_op jit(solution)/shard_map/while/body/eval_jaxpr/ppermute | solution.py:13
  30.5 5.8 %collective-permute-start = (bf16[128,256]{1,0:T(8,128)(2,1)}, bf16[128,256]{1,0:T(8,128)(2,1)S(1)}, u32[]{:S(2)}, u32[]{:S(2)}) collective-permute-start(bf16[128,256]{1,0:T(8,128)(2,1)} %get-tuple-element.331), channel_id=1, source_target_pairs={{0,8},{8,16},{16,24},{24,32},{32,40},{40,48},{48,56},{56,64},{64,7... | collective-permute-start | bytes 196616 | tf_op jit(solution)/shard_map/while/body/eval_jaxpr/ppermute | solution.py:13
  37.8 5.8 %collective-permute-start = (bf16[128,256]{1,0:T(8,128)(2,1)}, bf16[128,256]{1,0:T(8,128)(2,1)S(1)}, u32[]{:S(2)}, u32[]{:S(2)}) collective-permute-start(bf16[128,256]{1,0:T(8,128)(2,1)} %get-tuple-element.331), channel_id=1, source_target_pairs={{0,8},{8,16},{16,24},{24,32},{32,40},{40,48},{48,56},{56,64},{64,7... | collective-permute-start | bytes 196616 | tf_op jit(solution)/shard_map/while/body/eval_jaxpr/ppermute | solution.py:13
  45.0 5.8 %collective-permute-start = (bf16[128,256]{1,0:T(8,128)(2,1)}, bf16[128,256]{1,0:T(8,128)(2,1)S(1)}, u32[]{:S(2)}, u32[]{:S(2)}) collective-permute-start(bf16[128,256]{1,0:T(8,128)(2,1)} %get-tuple-element.331), channel_id=1, source_target_pairs={{0,8},{8,16},{16,24},{24,32},{32,40},{40,48},{48,56},{56,64},{64,7... | collective-permute-start | bytes 196616 | tf_op jit(solution)/shard_map/while/body/eval_jaxpr/ppermute | solution.py:13
  52.3 5.8 %collective-permute-start = (bf16[128,256]{1,0:T(8,128)(2,1)}, bf16[128,256]{1,0:T(8,128)(2,1)S(1)}, u32[]{:S(2)}, u32[]{:S(2)}) collective-permute-start(bf16[128,256]{1,0:T(8,128)(2,1)} %get-tuple-element.331), channel_id=1, source_target_pairs={{0,8},{8,16},{16,24},{24,32},{32,40},{40,48},{48,56},{56,64},{64,7... | collective-permute-start | bytes 196616 | tf_op jit(solution)/shard_map/while/body/eval_jaxpr/ppermute | solution.py:13
  59.5 5.8 %collective-permute-start = (bf16[128,256]{1,0:T(8,128)(2,1)}, bf16[128,256]{1,0:T(8,128)(2,1)S(1)}, u32[]{:S(2)}, u32[]{:S(2)}) collective-permute-start(bf16[128,256]{1,0:T(8,128)(2,1)} %get-tuple-element.331), channel_id=1, source_target_pairs={{0,8},{8,16},{16,24},{24,32},{32,40},{40,48},{48,56},{56,64},{64,7... | collective-permute-start | bytes 196616 | tf_op jit(solution)/shard_map/while/body/eval_jaxpr/ppermute | solution.py:13
  66.7 5.8 %collective-permute-start = (bf16[128,256]{1,0:T(8,128)(2,1)}, bf16[128,256]{1,0:T(8,128)(2,1)S(1)}, u32[]{:S(2)}, u32[]{:S(2)}) collective-permute-start(bf16[128,256]{1,0:T(8,128)(2,1)} %get-tuple-element.331), channel_id=1, source_target_pairs={{0,8},{8,16},{16,24},{24,32},{32,40},{40,48},{48,56},{56,64},{64,7... | collective-permute-start | bytes 196616 | tf_op jit(solution)/shard_map/while/body/eval_jaxpr/ppermute | solution.py:13
  74.0 5.8 %collective-permute-start = (bf16[128,256]{1,0:T(8,128)(2,1)}, bf16[128,256]{1,0:T(8,128)(2,1)S(1)}, u32[]{:S(2)}, u32[]{:S(2)}) collective-permute-start(bf16[128,256]{1,0:T(8,128)(2,1)} %get-tuple-element.331), channel_id=1, source_target_pairs={{0,8},{8,16},{16,24},{24,32},{32,40},{40,48},{48,56},{56,64},{64,7... | collective-permute-start | bytes 196616 | tf_op jit(solution)/shard_map/while/body/eval_jaxpr/ppermute | solution.py:13
  81.2 5.8 %collective-permute-start = (bf16[128,256]{1,0:T(8,128)(2,1)}, bf16[128,256]{1,0:T(8,128)(2,1)S(1)}, u32[]{:S(2)}, u32[]{:S(2)}) collective-permute-start(bf16[128,256]{1,0:T(8,128)(2,1)} %get-tuple-element.331), channel_id=1, source_target_pairs={{0,8},{8,16},{16,24},{24,32},{32,40},{40,48},{48,56},{56,64},{64,7... | collective-permute-start | bytes 196616 | tf_op jit(solution)/shard_map/while/body/eval_jaxpr/ppermute | solution.py:13
  88.5 5.8 %collective-permute-start = (bf16[128,256]{1,0:T(8,128)(2,1)}, bf16[128,256]{1,0:T(8,128)(2,1)S(1)}, u32[]{:S(2)}, u32[]{:S(2)}) collective-permute-start(bf16[128,256]{1,0:T(8,128)(2,1)} %get-tuple-element.331), channel_id=1, source_target_pairs={{0,8},{8,16},{16,24},{24,32},{32,40},{40,48},{48,56},{56,64},{64,7... | collective-permute-start | bytes 196616 | tf_op jit(solution)/shard_map/while/body/eval_jaxpr/ppermute | solution.py:13
  95.7 5.8 %collective-permute-start = (bf16[128,256]{1,0:T(8,128)(2,1)}, bf16[128,256]{1,0:T(8,128)(2,1)S(1)}, u32[]{:S(2)}, u32[]{:S(2)}) collective-permute-start(bf16[128,256]{1,0:T(8,128)(2,1)} %get-tuple-element.331), channel_id=1, source_target_pairs={{0,8},{8,16},{16,24},{24,32},{32,40},{40,48},{48,56},{56,64},{64,7... | collective-permute-start | bytes 196616 | tf_op jit(solution)/shard_map/while/body/eval_jaxpr/ppermute | solution.py:13
  103.0 7.6 %collective-permute-start = (bf16[128,256]{1,0:T(8,128)(2,1)}, bf16[128,256]{1,0:T(8,128)(2,1)S(1)}, u32[]{:S(2)}, u32[]{:S(2)}) collective-permute-start(bf16[128,256]{1,0:T(8,128)(2,1)} %get-tuple-element.331), channel_id=1, source_target_pairs={{0,8},{8,16},{16,24},{24,32},{32,40},{40,48},{48,56},{56,64},{64,7... | collective-permute-start | bytes 196616 | tf_op jit(solution)/shard_map/while/body/eval_jaxpr/ppermute | solution.py:13
  112.0 7.9 %collective-permute-start = (bf16[128,256]{1,0:T(8,128)(2,1)}, bf16[128,256]{1,0:T(8,128)(2,1)S(1)}, u32[]{:S(2)}, u32[]{:S(2)}) collective-permute-start(bf16[128,256]{1,0:T(8,128)(2,1)} %get-tuple-element.331), channel_id=1, source_target_pairs={{0,8},{8,16},{16,24},{24,32},{32,40},{40,48},{48,56},{56,64},{64,7... | collective-permute-start | bytes 196616 | tf_op jit(solution)/shard_map/while/body/eval_jaxpr/ppermute | solution.py:13
  121.3 33.3 %copy-start.3 = (bf16[16,3072]{1,0:T(8,128)(2,1)S(1)}, bf16[16,3072]{1,0:T(8,128)(2,1)}, u32[]{:S(2)}) copy-start(bf16[16,3072]{1,0:T(8,128)(2,1)} %param.18) | copy-start | bytes 294916
  122.3 13.8 %all-to-all-start = ((bf16[8,16,384]{2,1,0:T(8,128)(2,1)}), bf16[8,16,384]{2,1,0:T(8,128)(2,1)S(1)}, u32[]{:S(2)}, u32[]{:S(2)}) async-start(bf16[8,16,384]{2,1,0:T(8,128)(2,1)} %convert_element_type.88), calls=%async_computation | async-start | bytes 196608 | tf_op jit(solution)/shard_map/all_to_all | solution.py:76
  130.6 90.9 %all-gather.3.cloned.1.call-start = ((), (), s32[]{:S(2)}) async-start(), calls=%async_computation.7 | async-start | bytes 5013504 | tf_op jit(solution)/shard_map/all_gather | solution.py:98
  154.6 107.4 %all-gather.5.cloned.1.call-start = ((), (), s32[]{:S(2)}) async-start(), calls=%async_computation.9 | async-start | bytes 5013504 | tf_op jit(solution)/shard_map/all_gather | solution.py:127
  173.0 169.0 %reduce-scatter.3.cloned.1.call-start = ((), (), s32[]{:S(2)}) async-start(), calls=%async_computation.8 | async-start | bytes 5013504 | tf_op jit(solution)/shard_map/reduce_scatter | solution.py:105
  221.5 7.2 %copy-start.7 = (bf16[768,3072]{1,0:T(8,128)(2,1)S(1)}, bf16[768,3072]{1,0:T(8,128)(2,1)}, u32[]{:S(2)}) copy-start(bf16[768,3072]{1,0:T(8,128)(2,1)} %all-gather.3.cloned.1.call-done) | copy-start | bytes 14155780
  221.5 7.2 %copy-start.8 = (bf16[1,3072,512]{2,1,0:T(8,128)(2,1)S(1)}, bf16[1,3072,512]{2,1,0:T(8,128)(2,1)}, u32[]{:S(2)}) copy-start(bf16[1,3072,512]{2,1,0:T(8,128)(2,1)} %param.19) | copy-start | bytes 9437188
  269.0 0.9 copy-start.9
  274.2 136.7 %reduce-scatter.5.cloned.1.call-start = ((), (), s32[]{:S(2)}) async-start(), calls=%async_computation.10 | async-start | bytes 5013504 | tf_op jit(solution)/shard_map/reduce_scatter | solution.py:150
  274.4 4.9 %copy-start.1 = (bf16[1,3072,512]{2,1,0:T(8,128)(2,1)S(1)}, bf16[1,3072,512]{2,1,0:T(8,128)(2,1)}, u32[]{:S(2)}) copy-start(bf16[1,3072,512]{2,1,0:T(8,128)(2,1)} %param.20) | copy-start | bytes 9437188
  274.4 4.9 %copy-start.2 = (bf16[768,512]{1,0:T(8,128)(2,1)S(1)}, bf16[768,512]{1,0:T(8,128)(2,1)}, u32[]{:S(2)}) copy-start(bf16[768,512]{1,0:T(8,128)(2,1)} %get-tuple-element.248) | copy-start | bytes 2359300
  343.9 68.8 %all-to-all-start.2 = ((bf16[8,6,3072]{2,1,0:T(8,128)(2,1)}), bf16[8,6,3072]{2,1,0:T(8,128)(2,1)}, u32[]{:S(2)}, u32[]{:S(2)}) async-start(bf16[8,6,3072]{2,1,0:T(8,128)(2,1)} %reshape.130), calls=%async_computation.3 | async-start | bytes 786432 | tf_op jit(solution)/shard_map/all_to_all | solution.py:111
  412.7 18.1 %all-to-all-start.4 = ((bf16[8,6,3072]{2,1,0:T(8,128)(2,1)}), bf16[8,6,3072]{2,1,0:T(8,128)(2,1)}, u32[]{:S(2)}, u32[]{:S(2)}) async-start(bf16[8,6,3072]{2,1,0:T(8,128)(2,1)} %reshape.134), calls=%async_computation.6 | async-start | bytes 786432 | tf_op jit(solution)/shard_map/all_to_all | solution.py:161
Sparse Core Ops, SparseCore 0:
  154.7 66.6 all-gather.2
  223.7 38.2 all-gather.4
  274.3 67.7 reduce-scatter.2
  344.4 66.4 reduce-scatter.4
where the time goes:
time: 443 us; the launch traced here: 441 us
  waiting for transfers between devices  202 us (46%)
  starting transfers between devices  94.5 us (21%)
  matrix products  69.6 us (16%)
  local copies, waits for them, and re-layouts  27.4 us (6%)
  blocking collectives  27.3 us (6%)
  between operations  14 us (3%)
  other arithmetic  5.04 us (1%)
    ppermute x15, starting transfers between devices, shifted(): return lax.ppermute(block, axis, route)  70.9 us
    reduce_scatter x1, waiting for transfers between devices, local(): lax.psum_scatter((term + lax.dot_general(grad_up_pre, up_w, (((1,), (1,))...  52.4 us
    reduce_scatter x1, waiting for transfers between devices, local(): lax.psum_scatter(jnp.dot(hidden, down_w, preferred_element_type=jnp.float...  51.4 us
    all_gather x1, waiting for transfers between devices, local(): expert_in = lax.all_gather(arrived, 'ctx', axis=0, tiled=True)  48.4 us
    all_gather x1, waiting for transfers between devices, local(): lax.all_gather(grad_arrived, 'ctx', axis=0, tiled=True)  29.6 us
    ppermute x15, waiting for transfers between devices, shifted(): return lax.ppermute(block, axis, route)  15.6 us
    all_to_all x1, blocking collectives, local(): lax.all_to_all(send.reshape(n_exp, capacity, width), 'exp', split_axis=0,...  13.7 us
    all_to_all x1, blocking collectives, local(): lax.all_to_all(grad_slots.reshape(n_exp, capacity, width), 'exp', split_a...  13.6 us
  transfers between devices with their start and end apart: 22, of which 20 were waited for; matrix products, arithmetic and copies ran while one was open for 12% of the time, Pallas kernels for 0%

commit v1 on v0

--- a/solution.py
+++ b/solution.py
@@ -95,7 +95,9 @@
     arrived = lax.all_to_all(
         send.reshape(n_exp, capacity, width), "exp", split_axis=0, concat_axis=0, tiled=True
     ).reshape(slots, width)
-    expert_in = lax.all_gather(arrived, "ctx", axis=0, tiled=True)
+    expert_in = jnp.concatenate(
+        lax.all_to_all(jnp.stack([arrived] * lax.axis_size("ctx")), "ctx", 0, 0), axis=0
+    )
     gate_w = w_gate[0]
     up_w = w_up[0]
     down_w = w_down[0]

time: 443 us -> 484 us (1.093)
  blocking collectives: 27.3 us -> 134 us
  waiting for transfers between devices: 202 us -> 120 us
  matrix products: 69.6 us -> 78.7 us
  other arithmetic: 5.04 us -> 10.2 us
    all_to_all x1 -> x2, blocking collectives: 13.6 us -> 120 us  [the longest x1 109 us: local(): lax.all_to_all(jnp.stack([arrived] * lax.axis_size('ctx')), 'ctx', 0, 0)]
    all_gather x1, waiting for transfers between devices: 48.4 us -> 0.01 us  [local(): lax.all_gather(arrived, 'ctx', axis=0, tiled=True)]
    all_gather x1, waiting for transfers between devices: 29.6 us -> 0.01 us  [local(): lax.all_gather(grad_arrived, 'ctx', axis=0, tiled=True)]
    dot_general x16, matrix products: 4 us -> 17.4 us  [attend_piece(): lax.dot_general(query_flat, key_part, (((1,), (1,)), ((), ())), preferred...]
    reduce_scatter x1, waiting for transfers between devices: 52.4 us -> 47.4 us  [local(): lax.psum_scatter((term + lax.dot_general(grad_up_pre, up_w, (((1,), (1,))...]
  transfers between devices with their start and end apart: 22 -> 22, of which waited for: 20 -> 19; matrix products, arithmetic and copies ran while one was open for 12% -> 21% of each run, Pallas kernels for 0% -> 0%
where the time goes in v1:
time: 484 us; the launch traced here: 479 us
  blocking collectives  134 us (28%)
  waiting for transfers between devices  120 us (25%)
  starting transfers between devices  94.5 us (20%)
  matrix products  78.7 us (16%)
  local copies, waits for them, and re-layouts  27.1 us (6%)
  between operations  14 us (3%)
  other arithmetic  10.2 us (2%)
    all_to_all x1, blocking collectives, local(): lax.all_to_all(jnp.stack([arrived] * lax.axis_size('ctx')), 'ctx', 0, 0)  109 us
    ppermute x15, starting transfers between devices, shifted(): return lax.ppermute(block, axis, route)  71.1 us
    reduce_scatter x1, waiting for transfers between devices, local(): lax.psum_scatter(jnp.dot(hidden, down_w, preferred_element_type=jnp.float...  52.5 us
    reduce_scatter x1, waiting for transfers between devices, local(): lax.psum_scatter((term + lax.dot_general(grad_up_pre, up_w, (((1,), (1,))...  47.4 us
    dot_general x16, matrix products, attend_piece(): lax.dot_general(query_flat, key_part, (((1,), (1,)), ((), ())), preferred...  17.4 us
    ppermute x15, waiting for transfers between devices, shifted(): return lax.ppermute(block, axis, route)  15.6 us
    all_to_all x1, blocking collectives, local(): lax.all_to_all(send.reshape(n_exp, capacity, width), 'exp', split_axis=0,...  13.6 us
    all_to_all x1, blocking collectives, local(): lax.all_to_all(attended, 'exp', split_axis=0, concat_axis=1, tiled=True)  10.9 us
  transfers between devices with their start and end apart: 22, of which 19 were waited for; matrix products, arithmetic and copies ran while one was open for 21% of the time, Pallas kernels for 0%

profile of v1, /device:TPU:16, one launch (start us, length us, event | category | flops | bytes accessed | tf_op | source)
XLA Modules:
  0.0 479.3 jit_solution(10778050658558806661)
XLA Ops:
  11.5 1.3 convolution_convert_fusion.4
  13.7 8.3 %all-to-all-start.4 = ((bf16[8,6,3072]{2,1,0:T(8,128)(2,1)}), bf16[8,6,3072]{2,1,0:T(8,128)(2,1)}, u32[]{:S(2)}, u32[]{:S(2)}) async-start(bf16[8,6,3072]{2,1,0:T(8,128)(2,1)} %reshape.135), calls=%async_computation.5 | async-start | bytes 786432 | tf_op jit(solution)/shard_map/all_to_all | solution.py:125
  25.5 1.4 pad_maximum_fusion
  26.9 1.2 convolution_add_fusion.1
  29.3 1.8 reshape.136
  31.2 122.7 %while.22 = (s32[]{:T(128)}, f32[384]{0:T(512)S(1)}, f32[384]{0:T(512)S(1)}, f32[384,128]{1,0:T(8,128)S(1)}, bf16[128,256]{1,0:T(8,128)(2,1)}, /*index=5*/s32[]{...) while((s32[]{:T(128)}, f32[384]{0:T(512)S(1)}, ...), condition=%wide.region_11.12_spmd.clone, body=%wide.region_8.11_spmd.clone.sunk | while | flops 88720656 | bytes 1575218 | solution.py:67
  31.2 1.3 collective-permute-start
  36.0 4.7 collective-permute-start
  44.1 5.8 %collective-permute-start = (bf16[128,256]{1,0:T(8,128)(2,1)}, bf16[128,256]{1,0:T(8,128)(2,1)S(1)}, u32[]{:S(2)}, u32[]{:S(2)}) collective-permute-start(bf16[128,256]{1,0:T(8,128)(2,1)} %get-tuple-element.331), channel_id=1, source_target_pairs={{0,8},{8,16},{16,24},{24,32},{32,40},{40,48},{48,56},{56,64},{64,7... | collective-permute-start | bytes 196616 | tf_op jit(solution)/shard_map/while/body/eval_jaxpr/ppermute | solution.py:13
  53.3 6.1 %collective-permute-start = (bf16[128,256]{1,0:T(8,128)(2,1)}, bf16[128,256]{1,0:T(8,128)(2,1)S(1)}, u32[]{:S(2)}, u32[]{:S(2)}) collective-permute-start(bf16[128,256]{1,0:T(8,128)(2,1)} %get-tuple-element.331), channel_id=1, source_target_pairs={{0,8},{8,16},{16,24},{24,32},{32,40},{40,48},{48,56},{56,64},{64,7... | collective-permute-start | bytes 196616 | tf_op jit(solution)/shard_map/while/body/eval_jaxpr/ppermute | solution.py:13
  62.8 5.7 %collective-permute-start = (bf16[128,256]{1,0:T(8,128)(2,1)}, bf16[128,256]{1,0:T(8,128)(2,1)S(1)}, u32[]{:S(2)}, u32[]{:S(2)}) collective-permute-start(bf16[128,256]{1,0:T(8,128)(2,1)} %get-tuple-element.331), channel_id=1, source_target_pairs={{0,8},{8,16},{16,24},{24,32},{32,40},{40,48},{48,56},{56,64},{64,7... | collective-permute-start | bytes 196616 | tf_op jit(solution)/shard_map/while/body/eval_jaxpr/ppermute | solution.py:13
  72.0 4.8 %collective-permute-start = (bf16[128,256]{1,0:T(8,128)(2,1)}, bf16[128,256]{1,0:T(8,128)(2,1)S(1)}, u32[]{:S(2)}, u32[]{:S(2)}) collective-permute-start(bf16[128,256]{1,0:T(8,128)(2,1)} %get-tuple-element.331), channel_id=1, source_target_pairs={{0,8},{8,16},{16,24},{24,32},{32,40},{40,48},{48,56},{56,64},{64,7... | collective-permute-start | bytes 196616 | tf_op jit(solution)/shard_map/while/body/eval_jaxpr/ppermute | solution.py:13
  80.2 4.7 collective-permute-start
  88.4 4.7 collective-permute-start
  96.5 4.7 collective-permute-start
  104.6 4.7 collective-permute-start
  112.8 4.7 collective-permute-start
  120.9 4.7 collective-permute-start
  129.1 4.7 collective-permute-start
  137.2 4.7 collective-permute-start
  145.3 5.1 %collective-permute-start = (bf16[128,256]{1,0:T(8,128)(2,1)}, bf16[128,256]{1,0:T(8,128)(2,1)S(1)}, u32[]{:S(2)}, u32[]{:S(2)}) collective-permute-start(bf16[128,256]{1,0:T(8,128)(2,1)} %get-tuple-element.331), channel_id=1, source_target_pairs={{0,8},{8,16},{16,24},{24,32},{32,40},{40,48},{48,56},{56,64},{64,7... | collective-permute-start | bytes 196616 | tf_op jit(solution)/shard_map/while/body/eval_jaxpr/ppermute | solution.py:13
  154.2 10.9 %all_to_all.35 = bf16[8,16,384]{2,1,0:T(8,128)(2,1)S(1)} all-to-all(bf16[8,16,384]{2,1,0:T(8,128)(2,1)S(1)} %convert_element_type.88), channel_id=1, replica_groups=mesh['ctx'=16,'exp'=8] {'exp'}, dimensions={0} | all-to-all | bytes 196608 | tf_op jit(solution)/shard_map/all_to_all | solution.py:76
  166.3 1.8 reshape.131
  168.1 13.6 %all_to_all.36 = bf16[8,6,3072]{2,1,0:T(8,128)(2,1)} all-to-all(bf16[8,6,3072]{2,1,0:T(8,128)(2,1)} %reshape.131), channel_id=1, replica_groups=mesh['ctx'=16,'exp'=8] {'exp'}, dimensions={0} | all-to-all | bytes 589824 | tf_op jit(solution)/shard_map/all_to_all | solution.py:95
  181.7 1.8 stack_reshape.2
  183.6 1.5 stack.3
  185.2 109.3 %all_to_all.37 = bf16[16,48,3072]{2,1,0:T(8,128)(2,1)S(1)} all-to-all(bf16[16,48,3072]{2,1,0:T(8,128)(2,1)S(1)} %stack.3), channel_id=1, replica_groups=mesh['ctx'=16,'exp'=8] {'ctx'}, dimensions={0} | all-to-all | bytes 9437184 | tf_op jit(solution)/shard_map/all_to_all | solution.py:99
  294.5 3.7 fusion.18
  298.2 3.7 fusion.22
  302.0 7.0 %multiply_convert_fusion = (bf16[768,512]{1,0:T(8,128)(2,1)S(1)}, bf16[768,512]{1,0:T(8,128)(2,1)S(1)}, bf16[768,512]{1,0:T(8,128)(2,1)}) fusion(f32[768,512]{1,0:T(8,128)} %fusion.22, f32[768,512]{1,0:T(8,128)} %fusion.18, bf16[768,3072]{1,0:T(8,128)(2,1)} %all-gather.3.cloned.1.call-done, bf16[1,512,3072]{2,1,0:T(8,128)(2,1)S(1)} %copy-done), kind=kOutput, calls=%fused_computation.39 | convolution fusion | flops 2421817344 | bytes 13369344 | tf_op jit(solution)/shard_map/dot_general | solution.py:132
  309.0 2.6 fusion.20
  311.7 4.5 add_convert_fusion
  316.4 5.4 %convolution_convert_fusion = bf16[768,3072]{1,0:T(8,128)(2,1)} fusion(bf16[768,512]{1,0:T(8,128)(2,1)} %get-tuple-element.250, bf16[1,512,3072]{2,1,0:T(8,128)(2,1)S(1)} %copy-done), kind=kOutput, calls=%fused_computation.18 | convolution fusion | flops 2418278400 | bytes 8650752 | tf_op jit(solution)/shard_map/dot_general | solution.py:108
  321.9 6.9 %fusion.13 = bf16[1,512,3072]{2,1,0:T(8,128)(2,1)} fusion(bf16[768,512]{1,0:T(8,128)(2,1)} %get-tuple-element.250, bf16[768,3072]{1,0:T(8,128)(2,1)} %all-gather.3.cloned.1.call-done), kind=kOutput, calls=%fused_computation.24 | convolution fusion | flops 2417491968 | bytes 8650752 | tf_op jit(solution)/shard_map/dot_general | solution.py:135
  328.8 7.0 %fusion.11 = bf16[1,3072,512]{2,1,0:T(8,128)(2,1)} fusion(bf16[768,3072]{1,0:T(8,128)(2,1)} %all-gather.5.cloned.1.call-done, bf16[768,512]{1,0:T(8,128)(2,1)} %copy-done.14), kind=kOutput, calls=%fused_computation.22 | convolution fusion | flops 2417491968 | bytes 8650752 | tf_op jit(solution)/shard_map/dot_general | solution.py:143
  335.8 47.4 %reduce-scatter.5.cloned.1.call-done = bf16[48,3072]{1,0:T(8,128)(2,1)} async-done(((bf16[768,3072]{1,0:T(8,128)(2,1)}), bf16[48,3072]{1,0:T(8,128)(2,1)}) %reduce-scatter.5.cloned.1.call-update) | async-done | bytes 294928 | tf_op jit(solution)/shard_map/reduce_scatter | solution.py:152
  383.2 1.8 reshape.137
  385.0 7.4 %all-to-all-start.5 = ((bf16[8,6,3072]{2,1,0:T(8,128)(2,1)}), bf16[8,6,3072]{2,1,0:T(8,128)(2,1)}, u32[]{:S(2)}, u32[]{:S(2)}) async-start(bf16[8,6,3072]{2,1,0:T(8,128)(2,1)} %reshape.137), calls=%async_computation.7 | async-start | bytes 786432 | tf_op jit(solution)/shard_map/all_to_all | solution.py:163
  392.4 7.0 %fusion.12 = bf16[1,3072,512]{2,1,0:T(8,128)(2,1)} fusion(bf16[768,3072]{1,0:T(8,128)(2,1)} %all-gather.5.cloned.1.call-done, bf16[768,512]{1,0:T(8,128)(2,1)} %copy-done.3), kind=kOutput, calls=%fused_computation.23 | convolution fusion | flops 2417491968 | bytes 8650752 | tf_op jit(solution)/shard_map/dot_general | solution.py:146
  399.4 52.5 %reduce-scatter.3.cloned.1.call-done = bf16[48,3072]{1,0:T(8,128)(2,1)} async-done(((bf16[768,3072]{1,0:T(8,128)(2,1)}), bf16[48,3072]{1,0:T(8,128)(2,1)}) %reduce-scatter.3.cloned.1.call-update) | async-done | bytes 294928 | tf_op jit(solution)/shard_map/reduce_scatter | solution.py:107
  452.0 1.8 reshape.133
  453.8 7.4 %all-to-all-start.3 = ((bf16[8,6,3072]{2,1,0:T(8,128)(2,1)}), bf16[8,6,3072]{2,1,0:T(8,128)(2,1)}, u32[]{:S(2)}, u32[]{:S(2)}) async-start(bf16[8,6,3072]{2,1,0:T(8,128)(2,1)} %reshape.133), calls=%async_computation.4 | async-start | bytes 786432 | tf_op jit(solution)/shard_map/all_to_all | solution.py:113
  461.2 1.8 reshape.138
  463.0 1.3 multiply_reduce_fusion
  465.0 2.8 all-to-all-done.3
  467.8 1.8 reshape.134
  469.6 1.9 convolution_convert_fusion.6
  471.5 1.3 subtract_convert_fusion
  (222 shorter events, 62.7 us)
Async XLA Ops:
  7.2 294.8 %copy-start = (bf16[1,512,3072]{2,1,0:T(8,128)(2,1)S(1)}, bf16[1,512,3072]{2,1,0:T(8,128)(2,1)}, u32[]{:S(2)}) copy-start(bf16[1,512,3072]{2,1,0:T(8,128)(2,1)} %param.21) | copy-start | bytes 9437188
  11.5 11.7 %copy-start.5 = (f32[48,16]{0,1:T(8,128)}, f32[48,16]{0,1:T(8,128)S(1)}, u32[]{:S(2)}) copy-start(f32[48,16]{0,1:T(8,128)S(1)} %get-tuple-element.227) | copy-start | bytes 9220
  13.7 15.6 %all-to-all-start.4 = ((bf16[8,6,3072]{2,1,0:T(8,128)(2,1)}), bf16[8,6,3072]{2,1,0:T(8,128)(2,1)}, u32[]{:S(2)}, u32[]{:S(2)}) async-start(bf16[8,6,3072]{2,1,0:T(8,128)(2,1)} %reshape.135), calls=%async_computation.5 | async-start | bytes 786432 | tf_op jit(solution)/shard_map/all_to_all | solution.py:125
  22.0 280.0 %all-gather.3.cloned.1.call-start = ((), (), s32[]{:S(2)}) async-start(), calls=%async_computation.9 | async-start | bytes 5013504 | tf_op jit(solution)/shard_map/all_gather | solution.py:129
  22.0 2.2 copy-start.8
  22.0 2.2 copy-start.9
  23.2 3.8 copy-start.4
  31.2 297.7 %all-gather.5.cloned.1.call-start = ((), (), s32[]{:S(2)}) async-start(), calls=%async_computation.11 | async-start | bytes 5013504 | tf_op jit(solution)/shard_map/all_gather | solution.py:130
  31.2 134.1 %copy-start.7 = (f32[3072]{0:T(1024)S(1)}, f32[3072]{0:T(1024)}, u32[]{:S(2)}) copy-start(f32[3072]{0:T(1024)} %param.15) | copy-start | bytes 36868
  31.2 2.4 collective-permute-start
  36.0 5.8 %collective-permute-start = (bf16[128,256]{1,0:T(8,128)(2,1)}, bf16[128,256]{1,0:T(8,128)(2,1)S(1)}, u32[]{:S(2)}, u32[]{:S(2)}) collective-permute-start(bf16[128,256]{1,0:T(8,128)(2,1)} %get-tuple-element.331), channel_id=1, source_target_pairs={{0,8},{8,16},{16,24},{24,32},{32,40},{40,48},{48,56},{56,64},{64,7... | collective-permute-start | bytes 196616 | tf_op jit(solution)/shard_map/while/body/eval_jaxpr/ppermute | solution.py:13
  44.1 6.9 %collective-permute-start = (bf16[128,256]{1,0:T(8,128)(2,1)}, bf16[128,256]{1,0:T(8,128)(2,1)S(1)}, u32[]{:S(2)}, u32[]{:S(2)}) collective-permute-start(bf16[128,256]{1,0:T(8,128)(2,1)} %get-tuple-element.331), channel_id=1, source_target_pairs={{0,8},{8,16},{16,24},{24,32},{32,40},{40,48},{48,56},{56,64},{64,7... | collective-permute-start | bytes 196616 | tf_op jit(solution)/shard_map/while/body/eval_jaxpr/ppermute | solution.py:13
  53.3 7.2 %collective-permute-start = (bf16[128,256]{1,0:T(8,128)(2,1)}, bf16[128,256]{1,0:T(8,128)(2,1)S(1)}, u32[]{:S(2)}, u32[]{:S(2)}) collective-permute-start(bf16[128,256]{1,0:T(8,128)(2,1)} %get-tuple-element.331), channel_id=1, source_target_pairs={{0,8},{8,16},{16,24},{24,32},{32,40},{40,48},{48,56},{56,64},{64,7... | collective-permute-start | bytes 196616 | tf_op jit(solution)/shard_map/while/body/eval_jaxpr/ppermute | solution.py:13
  62.8 6.8 %collective-permute-start = (bf16[128,256]{1,0:T(8,128)(2,1)}, bf16[128,256]{1,0:T(8,128)(2,1)S(1)}, u32[]{:S(2)}, u32[]{:S(2)}) collective-permute-start(bf16[128,256]{1,0:T(8,128)(2,1)} %get-tuple-element.331), channel_id=1, source_target_pairs={{0,8},{8,16},{16,24},{24,32},{32,40},{40,48},{48,56},{56,64},{64,7... | collective-permute-start | bytes 196616 | tf_op jit(solution)/shard_map/while/body/eval_jaxpr/ppermute | solution.py:13
  72.0 5.9 %collective-permute-start = (bf16[128,256]{1,0:T(8,128)(2,1)}, bf16[128,256]{1,0:T(8,128)(2,1)S(1)}, u32[]{:S(2)}, u32[]{:S(2)}) collective-permute-start(bf16[128,256]{1,0:T(8,128)(2,1)} %get-tuple-element.331), channel_id=1, source_target_pairs={{0,8},{8,16},{16,24},{24,32},{32,40},{40,48},{48,56},{56,64},{64,7... | collective-permute-start | bytes 196616 | tf_op jit(solution)/shard_map/while/body/eval_jaxpr/ppermute | solution.py:13
  80.2 5.8 %collective-permute-start = (bf16[128,256]{1,0:T(8,128)(2,1)}, bf16[128,256]{1,0:T(8,128)(2,1)S(1)}, u32[]{:S(2)}, u32[]{:S(2)}) collective-permute-start(bf16[128,256]{1,0:T(8,128)(2,1)} %get-tuple-element.331), channel_id=1, source_target_pairs={{0,8},{8,16},{16,24},{24,32},{32,40},{40,48},{48,56},{56,64},{64,7... | collective-permute-start | bytes 196616 | tf_op jit(solution)/shard_map/while/body/eval_jaxpr/ppermute | solution.py:13
  88.4 5.8 %collective-permute-start = (bf16[128,256]{1,0:T(8,128)(2,1)}, bf16[128,256]{1,0:T(8,128)(2,1)S(1)}, u32[]{:S(2)}, u32[]{:S(2)}) collective-permute-start(bf16[128,256]{1,0:T(8,128)(2,1)} %get-tuple-element.331), channel_id=1, source_target_pairs={{0,8},{8,16},{16,24},{24,32},{32,40},{40,48},{48,56},{56,64},{64,7... | collective-permute-start | bytes 196616 | tf_op jit(solution)/shard_map/while/body/eval_jaxpr/ppermute | solution.py:13
  96.5 5.8 %collective-permute-start = (bf16[128,256]{1,0:T(8,128)(2,1)}, bf16[128,256]{1,0:T(8,128)(2,1)S(1)}, u32[]{:S(2)}, u32[]{:S(2)}) collective-permute-start(bf16[128,256]{1,0:T(8,128)(2,1)} %get-tuple-element.331), channel_id=1, source_target_pairs={{0,8},{8,16},{16,24},{24,32},{32,40},{40,48},{48,56},{56,64},{64,7... | collective-permute-start | bytes 196616 | tf_op jit(solution)/shard_map/while/body/eval_jaxpr/ppermute | solution.py:13
  104.6 5.8 %collective-permute-start = (bf16[128,256]{1,0:T(8,128)(2,1)}, bf16[128,256]{1,0:T(8,128)(2,1)S(1)}, u32[]{:S(2)}, u32[]{:S(2)}) collective-permute-start(bf16[128,256]{1,0:T(8,128)(2,1)} %get-tuple-element.331), channel_id=1, source_target_pairs={{0,8},{8,16},{16,24},{24,32},{32,40},{40,48},{48,56},{56,64},{64,7... | collective-permute-start | bytes 196616 | tf_op jit(solution)/shard_map/while/body/eval_jaxpr/ppermute | solution.py:13
  112.8 5.8 %collective-permute-start = (bf16[128,256]{1,0:T(8,128)(2,1)}, bf16[128,256]{1,0:T(8,128)(2,1)S(1)}, u32[]{:S(2)}, u32[]{:S(2)}) collective-permute-start(bf16[128,256]{1,0:T(8,128)(2,1)} %get-tuple-element.331), channel_id=1, source_target_pairs={{0,8},{8,16},{16,24},{24,32},{32,40},{40,48},{48,56},{56,64},{64,7... | collective-permute-start | bytes 196616 | tf_op jit(solution)/shard_map/while/body/eval_jaxpr/ppermute | solution.py:13
  120.9 5.8 %collective-permute-start = (bf16[128,256]{1,0:T(8,128)(2,1)}, bf16[128,256]{1,0:T(8,128)(2,1)S(1)}, u32[]{:S(2)}, u32[]{:S(2)}) collective-permute-start(bf16[128,256]{1,0:T(8,128)(2,1)} %get-tuple-element.331), channel_id=1, source_target_pairs={{0,8},{8,16},{16,24},{24,32},{32,40},{40,48},{48,56},{56,64},{64,7... | collective-permute-start | bytes 196616 | tf_op jit(solution)/shard_map/while/body/eval_jaxpr/ppermute | solution.py:13
  129.1 5.8 %collective-permute-start = (bf16[128,256]{1,0:T(8,128)(2,1)}, bf16[128,256]{1,0:T(8,128)(2,1)S(1)}, u32[]{:S(2)}, u32[]{:S(2)}) collective-permute-start(bf16[128,256]{1,0:T(8,128)(2,1)} %get-tuple-element.331), channel_id=1, source_target_pairs={{0,8},{8,16},{16,24},{24,32},{32,40},{40,48},{48,56},{56,64},{64,7... | collective-permute-start | bytes 196616 | tf_op jit(solution)/shard_map/while/body/eval_jaxpr/ppermute | solution.py:13
  137.2 5.8 %collective-permute-start = (bf16[128,256]{1,0:T(8,128)(2,1)}, bf16[128,256]{1,0:T(8,128)(2,1)S(1)}, u32[]{:S(2)}, u32[]{:S(2)}) collective-permute-start(bf16[128,256]{1,0:T(8,128)(2,1)} %get-tuple-element.331), channel_id=1, source_target_pairs={{0,8},{8,16},{16,24},{24,32},{32,40},{40,48},{48,56},{56,64},{64,7... | collective-permute-start | bytes 196616 | tf_op jit(solution)/shard_map/while/body/eval_jaxpr/ppermute | solution.py:13
  145.3 6.2 %collective-permute-start = (bf16[128,256]{1,0:T(8,128)(2,1)}, bf16[128,256]{1,0:T(8,128)(2,1)S(1)}, u32[]{:S(2)}, u32[]{:S(2)}) collective-permute-start(bf16[128,256]{1,0:T(8,128)(2,1)} %get-tuple-element.331), channel_id=1, source_target_pairs={{0,8},{8,16},{16,24},{24,32},{32,40},{40,48},{48,56},{56,64},{64,7... | collective-permute-start | bytes 196616 | tf_op jit(solution)/shard_map/while/body/eval_jaxpr/ppermute | solution.py:13
  165.3 19.9 %copy-start.11 = (f32[16]{0:T(128)}, f32[16]{0:T(128)S(1)}, u32[]{:S(2)}) copy-start(f32[16]{0:T(128)S(1)} %fusion.26) | copy-start | bytes 196
  165.3 19.9 %copy-start.10 = (f32[16]{0:T(128)}, f32[16]{0:T(128)S(1)}, u32[]{:S(2)}) copy-start(f32[16]{0:T(128)S(1)} %add_rsqrt_fusion) | copy-start | bytes 196
  183.6 199.6 %reduce-scatter.5.cloned.1.call-start = ((), (), s32[]{:S(2)}) async-start(), calls=%async_computation.10 | async-start | bytes 5013504 | tf_op jit(solution)/shard_map/reduce_scatter | solution.py:152
  185.2 109.3 %copy-start.1 = (bf16[1,3072,512]{2,1,0:T(8,128)(2,1)S(1)}, bf16[1,3072,512]{2,1,0:T(8,128)(2,1)}, u32[]{:S(2)}) copy-start(bf16[1,3072,512]{2,1,0:T(8,128)(2,1)} %param.20) | copy-start | bytes 9437188
  294.5 3.7 copy-start.12
  302.0 7.0 %copy-start.13 = (bf16[1,3072,512]{2,1,0:T(8,128)(2,1)S(1)}, bf16[1,3072,512]{2,1,0:T(8,128)(2,1)}, u32[]{:S(2)}) copy-start(bf16[1,3072,512]{2,1,0:T(8,128)(2,1)} %param.19) | copy-start | bytes 9437188
  309.0 2.7 copy-start.14
  309.0 2.7 copy-start.3
  309.0 2.7 copy-start.2
  316.2 135.8 %reduce-scatter.3.cloned.1.call-start = ((), (), s32[]{:S(2)}) async-start(), calls=%async_computation.8 | async-start | bytes 5013504 | tf_op jit(solution)/shard_map/reduce_scatter | solution.py:107
  385.0 68.8 %all-to-all-start.5 = ((bf16[8,6,3072]{2,1,0:T(8,128)(2,1)}), bf16[8,6,3072]{2,1,0:T(8,128)(2,1)}, u32[]{:S(2)}, u32[]{:S(2)}) async-start(bf16[8,6,3072]{2,1,0:T(8,128)(2,1)} %reshape.137), calls=%async_computation.7 | async-start | bytes 786432 | tf_op jit(solution)/shard_map/all_to_all | solution.py:163
  399.4 70.2 %copy-start.6 = (f32[48,16]{0,1:T(8,128)S(1)}, f32[48,16]{0,1:T(8,128)}, u32[]{:S(2)}) copy-start(f32[48,16]{0,1:T(8,128)} %copy-done.5) | copy-start | bytes 9220
  453.8 14.1 %all-to-all-start.3 = ((bf16[8,6,3072]{2,1,0:T(8,128)(2,1)}), bf16[8,6,3072]{2,1,0:T(8,128)(2,1)}, u32[]{:S(2)}, u32[]{:S(2)}) async-start(bf16[8,6,3072]{2,1,0:T(8,128)(2,1)} %reshape.133), calls=%async_computation.4 | async-start | bytes 786432 | tf_op jit(solution)/shard_map/all_to_all | solution.py:113
Sparse Core Ops, SparseCore 0:
  31.3 38.4 all-gather.2
  183.7 112.9 all-gather.4
  316.3 66.8 reduce-scatter.4
  385.5 66.4 reduce-scatter.2
